TPU v7x, 32 devices: a whole 2x2x4 slice. The times are simulated.
32 devices in a mesh: side: 2 (over core), group: 8 (over z, y), head: 2 (over x).
Axes of the slice: x: 2, y: 2, z: 4, core: 2. Of those that a mesh axis runs over, the one named last changes fastest.
Arguments:
- pool_rows: bfloat16 [2, 768, 4096], P('side', ('group', 'head')), may hold values from -24 to 24
- pool_weight: bfloat16 [2, 4096, 8192], P('side', 'group', 'head'), as said below
- lengths: int32 [8, 3], replicated, may hold values from 1 to 48, 96 in all within a row
- owner: int32 [8, 3], replicated, may hold values from 0 to 7, as said below
Outputs:
- pool_out: bfloat16 [2, 768, 4096], P('side', 'group', 'head')
Inputs may be any that keep to these rules, and one draw needn't show every extreme that they name: owner[p, j] is p with the binary digits of m_j flipped, where m_j = owner[0, j] is the same for every p; the m_j differ between slots, and every binary digit below 8 is set in some m_j. So the 3 requests of a prefill group go to different decode groups, and every decode group receives exactly one request for each slot j. `lengths`: each row sums to 96. `pool_weight`: independent normal entries of deviation 1 / sqrt(4096).
All inputs are finite; a program needn't handle non-finite values.
Results may differ from a plain program's by a relative error of at most 0.0061.
Values may be sent and summed in bfloat16 or wider, within the bound.
A program may use at most 128 MiB of HBM per device.

v0:
```python
import jax
import jax.numpy as jnp
from jax import lax
from jax.sharding import PartitionSpec as P

HEAD_DIM = 256


def shifted(value, axis, by):
    count = lax.axis_size(axis)
    pairs = [(i, i + by) for i in range(count) if 0 <= i + by < count]
    return lax.ppermute(value, axis, pairs)


def on_device(pool_rows, pool_weight, lengths, owner):
    side_index = lax.axis_index("side")
    group_index = lax.axis_index("group")
    requests = lengths.shape[1]
    gathered = lax.all_gather(pool_rows[0], "head", axis=0, tiled=True)
    weight = lax.all_gather(pool_weight[0], "group", axis=0, tiled=True)
    mem_g = gathered.shape[0]
    wide = weight.shape[1] // 2
    heads_dev = wide // HEAD_DIM
    q_req = mem_g // requests
    scale = 1.0 / HEAD_DIM**0.5
    cached = jnp.dot(gathered, weight, preferred_element_type=jnp.float32).astype(jnp.bfloat16)
    queries = cached[:, :wide]
    starts = jnp.cumsum(lengths, axis=1) - lengths
    groups = jnp.arange(lengths.shape[0], dtype=jnp.int32)
    sources, begins, counts = ([], [], [])
    for slot in range(requests):
        hit = owner[:, slot] == group_index
        sources.append(jnp.sum(jnp.where(hit, groups, 0)))
        begins.append(jnp.sum(jnp.where(hit, starts[:, slot], 0)))
        counts.append(jnp.sum(jnp.where(hit, lengths[:, slot], 0)))
    moved = shifted(cached, "side", 1)
    row_slot = jnp.arange(mem_g, dtype=jnp.int32) // q_req
    lower = jnp.zeros((mem_g,), jnp.int32)
    upper = jnp.zeros((mem_g,), jnp.int32)
    for slot in range(requests):
        here = row_slot == slot
        first_row = sources[slot] * mem_g + begins[slot]
        lower = jnp.where(here, first_row, lower)
        upper = jnp.where(here, first_row + counts[slot], upper)
    query_heads = queries.reshape(mem_g, heads_dev, HEAD_DIM)
    piece = lax.all_gather(moved, "group", axis=0, tiled=True)
    running = jnp.full((heads_dev, mem_g), -1e30, jnp.float32)
    count_rows = piece.shape[0]
    key_index = jnp.arange(count_rows, dtype=jnp.int32)
    key_rows = piece[:, :wide].reshape(count_rows, heads_dev, HEAD_DIM)
    value_rows = piece[:, wide:].reshape(count_rows, heads_dev, HEAD_DIM)
    allowed = (key_index[None, :] >= lower[:, None]) & (key_index[None, :] < upper[:, None])
    scores = (
        jnp.einsum("qeh,keh->eqk", query_heads, key_rows, preferred_element_type=jnp.float32)
        * scale
    )
    scores = jnp.where(allowed[None], scores, -1e30)
    newest = jnp.maximum(running, jnp.max(scores, axis=-1))
    expo = jnp.where(allowed[None], jnp.exp(scores - newest[:, :, None]), 0.0)
    total = jnp.sum(expo, axis=-1)
    update = jnp.einsum(
        "eqk,keh->eqh", expo.astype(jnp.bfloat16), value_rows, preferred_element_type=jnp.float32
    )
    accum = update
    running, total, accum = (newest, total, accum)
    mixed = accum / total[:, :, None]
    attended = jnp.transpose(mixed, (1, 0, 2)).reshape(mem_g, wide).astype(jnp.bfloat16)
    partial_out = lax.dot_general(
        attended, weight[:, wide:], (((1,), (1,)), ((), ())), preferred_element_type=jnp.float32
    )
    decoded = lax.psum_scatter(partial_out, "head", scatter_dimension=1, tiled=True).astype(
        jnp.bfloat16
    )
    result = jnp.where(side_index == 0, cached[:, :wide], decoded)
    return result[None]


def solution(mesh):
    placed = (P("side", ("group", "head"), None), P("side", "group", "head"), P(), P())
    return jax.shard_map(
        on_device, mesh=mesh, in_specs=placed, out_specs=P("side", "group", "head"), check_vma=False
    )
```

profile of v0, /device:TPU:0, one launch (start us, length us, event | category | flops | bytes accessed | tf_op | source)
XLA Modules:
  0.0 815.8 jit_solution(10971161938531449910)
XLA Ops:
  6.5 0.0 copy-start.1
  6.5 0.0 all-gather.7.cloned.1.call-start
  6.5 0.7 all-gather.7.cloned.1.call-update
  7.3 0.0 all-gather.5.cloned.1.call-start
  7.3 0.2 copy-done.1
  7.5 12.7 %all-gather = bf16[1,96,4096]{2,1,0:T(8,128)(2,1)S(1)} all-gather(bf16[1,48,4096]{2,1,0:T(8,128)(2,1)S(1)} %copy-done.1), channel_id=2, replica_groups=mesh['side'=2,'group'=8,'head'=2] {'head'}, dimensions={1}, use_global_device_ids=true | all-gather | bytes 1179648 | tf_op jit(solution)/shard_map/all_gather | solution.py:19
  20.3 0.0 copy-start.2
  20.3 0.0 copy-start.3
  20.3 629.0 %all-gather.7.cloned.1.call-done = bf16[1,4096,4096]{2,1,0:T(8,128)(2,1)} async-done(((bf16[1,512,4096]{2,1,0:T(8,128)(2,1)}), bf16[1,4096,4096]{2,1,0:T(8,128)(2,1)}) %all-gather.7.cloned.1.call-update) | async-done | bytes 33554448 | tf_op jit(solution)/shard_map/all_gather | solution.py:20
  649.3 13.4 %convolution_convert_fusion = bf16[96,4096]{1,0:T(8,128)(2,1)S(1)} fusion(bf16[1,96,4096]{2,1,0:T(8,128)(2,1)S(1)} %all-gather, bf16[1,4096,4096]{2,1,0:T(8,128)(2,1)} %all-gather.7.cloned.1.call-done), kind=kOutput, calls=%fused_computation.2 | convolution fusion | flops 3221618688 | bytes 35127296 | tf_op jit(solution)/shard_map/dot_general | solution.py:26
  662.7 1.6 collective-permute-start
  664.3 1.8 collective-permute-done
  666.2 0.0 copy-start
  666.2 0.9 copy-done
  667.1 0.0 all-gather.5.cloned.1.call-update
  667.1 0.0 reduce-scatter.2.cloned.1.call-start
  667.2 0.0 copy-done.2
  667.2 0.0 copy-done.3
  667.2 0.8 fusion.41
  673.7 0.1 fusion.38
  673.9 92.4 %all-gather.5.cloned.1.call-done = bf16[768,4096]{1,0:T(8,128)(2,1)} async-done(((bf16[96,4096]{1,0:T(8,128)(2,1)}), bf16[768,4096]{1,0:T(8,128)(2,1)}) %all-gather.5.cloned.1.call-update) | async-done | bytes 6291472 | tf_op jit(solution)/shard_map/all_gather | solution.py:46
  766.3 3.4 fusion.52
  769.8 1.2 fusion.8
  771.0 0.8 fusion.9
  771.7 1.1 fusion.30
  772.9 9.9 %fusion = f32[96,4096]{1,0:T(8,128)} fusion(bf16[96,2048]{1,0:T(8,128)(2,1)S(1)} %bitcast.91, bf16[4096,4096]{1,0:T(8,128)(2,1)} %bitcast.87), kind=kOutput, calls=%fused_computation | convolution fusion | flops 1610612736 | bytes 18743296 | tf_op jit(solution)/shard_map/dot_general | solution.py:68
  782.8 0.0 reduce-scatter.2.cloned.1.call-update
  782.8 24.5 %reduce-scatter.2.cloned.1.call-done = f32[96,2048]{1,0:T(8,128)} async-done(((f32[96,4096]{1,0:T(8,128)}), f32[96,2048]{1,0:T(8,128)}) %reduce-scatter.2.cloned.1.call-update) | async-done | bytes 786448 | tf_op jit(solution)/shard_map/reduce_scatter | solution.py:71
  807.3 1.9 select_bitcast_fusion
  (6 shorter events, 0.1 us)
Async XLA Ops:
  6.5 1.0 copy-start.1
  6.5 642.8 %all-gather.7.cloned.1.call-start = ((), (), s32[]{:S(2)}) async-start(), calls=%async_computation.3 | async-start | bytes 37748736 | tf_op jit(solution)/shard_map/all_gather | solution.py:20
  7.3 759.1 %all-gather.5.cloned.1.call-start = ((), (), s32[]{:S(2)}) async-start(), calls=%async_computation.1 | async-start | bytes 7077888 | tf_op jit(solution)/shard_map/all_gather | solution.py:46
  20.3 646.9 %copy-start.2 = (s32[8,3]{0,1:T(4,128)S(1)}, s32[8,3]{0,1:T(4,128)}, u32[]{:S(2)}) copy-start(s32[8,3]{0,1:T(4,128)} %param.6) | copy-start | bytes 292
  20.3 647.0 %copy-start.3 = (s32[8,3]{0,1:T(4,128)S(1)}, s32[8,3]{0,1:T(4,128)}, u32[]{:S(2)}) copy-start(s32[8,3]{0,1:T(4,128)} %param.7) | copy-start | bytes 292
  662.7 3.5 collective-permute-start
  666.2 0.9 copy-start
  667.1 140.2 %reduce-scatter.2.cloned.1.call-start = ((), (), s32[]{:S(2)}) async-start(), calls=%async_computation.2 | async-start | bytes 2359296 | tf_op jit(solution)/shard_map/reduce_scatter | solution.py:71
Sparse Core Ops, SparseCore 0:
  8.9 640.3 all-gather.6
  667.3 99.0 all-gather.4
  782.9 24.3 reduce-scatter.1
where the time goes:
time: 816 us
  waiting for transfers between devices  749 us (92%)
  matrix products  25.6 us (3%)
  between operations  18.8 us (2%)
  blocking collectives  12.7 us (2%)
    all_gather x1, waiting for transfers between devices, on_device(): weight = lax.all_gather(pool_weight[0], 'group', axis=0, tiled=True)  629 us
    all_gather x1, waiting for transfers between devices, on_device(): piece = lax.all_gather(moved, 'group', axis=0, tiled=True)  92.4 us
    reduce_scatter x1, waiting for transfers between devices, on_device(): lax.psum_scatter(partial_out, 'head', scatter_dimension=1, tiled=True)  24.5 us
  transfers between devices with their start and end apart: 4, of which 4 were waited for; matrix products, arithmetic and copies ran while one was open for 0% of the time, Pallas kernels for 0%

commit v1 on v0

--- a/solution.py
+++ b/solution.py
@@ -43,7 +43,9 @@
         lower = jnp.where(here, first_row, lower)
         upper = jnp.where(here, first_row + counts[slot], upper)
     query_heads = queries.reshape(mem_g, heads_dev, HEAD_DIM)
-    piece = lax.all_gather(moved, "group", axis=0, tiled=True)
+    piece = jnp.concatenate(
+        lax.all_to_all(jnp.stack([moved] * lax.axis_size("group")), "group", 0, 0), axis=0
+    )
     running = jnp.full((heads_dev, mem_g), -1e30, jnp.float32)
     count_rows = piece.shape[0]
     key_index = jnp.arange(count_rows, dtype=jnp.int32)

time: 816 us -> 873 us (1.070)
  waiting for transfers between devices: 749 us -> 788 us
  local copies, waits for them, and re-layouts: 4.64 us -> 15.1 us
    all_to_all x0 -> x1, waiting for transfers between devices: none -> 131 us  [on_device(): lax.all_to_all(jnp.stack([moved] * lax.axis_size('group')), 'group', 0, 0)]
    all_gather x1 -> x0, waiting for transfers between devices: 92.4 us -> none  [on_device(): piece = lax.all_gather(moved, 'group', axis=0, tiled=True)]
where the time goes in v1:
time: 873 us
  waiting for transfers between devices  788 us (90%)
  matrix products  26.4 us (3%)
  between operations  19.3 us (2%)
  local copies, waits for them, and re-layouts  15.1 us (2%)
  blocking collectives  12.7 us (1%)
    all_gather x1, waiting for transfers between devices, on_device(): weight = lax.all_gather(pool_weight[0], 'group', axis=0, tiled=True)  629 us
    all_to_all x1, waiting for transfers between devices, on_device(): lax.all_to_all(jnp.stack([moved] * lax.axis_size('group')), 'group', 0, 0)  131 us
    reduce_scatter x1, waiting for transfers between devices, on_device(): lax.psum_scatter(partial_out, 'head', scatter_dimension=1, tiled=True)  25.3 us
  transfers between devices with their start and end apart: 4, of which 4 were waited for; matrix products, arithmetic and copies ran while one was open for 0% of the time, Pallas kernels for 0%

profile of v1, /device:TPU:0, one launch (start us, length us, event | category | flops | bytes accessed | tf_op | source)
XLA Modules:
  0.0 872.8 jit_solution(16257340204348055478)
XLA Ops:
  6.5 0.0 all-gather.4.cloned.1.call-start
  6.5 0.7 all-gather.4.cloned.1.call-update
  7.3 0.3 copy-done.4
  7.5 12.7 %all-gather = bf16[1,96,4096]{2,1,0:T(8,128)(2,1)S(1)} all-gather(bf16[1,48,4096]{2,1,0:T(8,128)(2,1)S(1)} %copy-done.4), channel_id=2, replica_groups=mesh['side'=2,'group'=8,'head'=2] {'head'}, dimensions={1}, use_global_device_ids=true | all-gather | bytes 1179648 | tf_op jit(solution)/shard_map/all_gather | solution.py:19
  20.3 629.0 %all-gather.4.cloned.1.call-done = bf16[1,4096,4096]{2,1,0:T(8,128)(2,1)} async-done(((bf16[1,512,4096]{2,1,0:T(8,128)(2,1)}), bf16[1,4096,4096]{2,1,0:T(8,128)(2,1)}) %all-gather.4.cloned.1.call-update) | async-done | bytes 33554448 | tf_op jit(solution)/shard_map/all_gather | solution.py:20
  649.3 13.4 %convolution_convert_fusion = bf16[96,4096]{1,0:T(8,128)(2,1)S(1)} fusion(bf16[1,96,4096]{2,1,0:T(8,128)(2,1)S(1)} %all-gather, bf16[1,4096,4096]{2,1,0:T(8,128)(2,1)} %all-gather.4.cloned.1.call-done), kind=kOutput, calls=%fused_computation.2 | convolution fusion | flops 3221618688 | bytes 35127296 | tf_op jit(solution)/shard_map/dot_general | solution.py:26
  662.7 0.0 copy-start.1
  662.7 1.6 collective-permute-start
  664.4 1.8 collective-permute-done
  666.2 3.4 stack.2
  669.6 5.0 all-to-all-start
  674.6 0.0 reduce-scatter.2.cloned.1.call-start
  674.7 0.0 copy-done.5
  674.7 0.0 copy-done.6
  674.7 0.8 fusion.21
  681.3 0.8 fusion.18
  682.1 0.0 copy-done.1
  682.1 131.3 %all-to-all-done = bf16[8,96,4096]{2,1,0:T(8,128)(2,1)} async-done(((bf16[8,96,4096]{2,1,0:T(8,128)(2,1)}), bf16[8,96,4096]{2,1,0:T(8,128)(2,1)}, u32[]{:S(2)}, u32[]{:S(2)}) %all-to-all-start) | async-done | bytes 6291488 | tf_op jit(solution)/shard_map/all_to_all | solution.py:47
  813.5 5.4 fusion.32
  818.9 2.8 copy.14
  821.7 3.2 copy.11
  824.9 0.0 copy-start.3
  824.9 0.0 copy-start
  824.9 1.8 fusion.2
  826.7 0.0 copy-done.3
  826.7 0.7 fusion.3
  827.5 1.2 fusion.7
  828.7 10.0 %fusion = f32[96,4096]{1,0:T(8,128)} fusion(bf16[96,2048]{1,0:T(8,128)(2,1)S(1)} %bitcast.78, bf16[4096,4096]{1,0:T(8,128)(2,1)} %bitcast.74), kind=kOutput, calls=%fused_computation | convolution fusion | flops 1610612736 | bytes 18743296 | tf_op jit(solution)/shard_map/dot_general | solution.py:70
  838.7 0.0 reduce-scatter.2.cloned.1.call-update
  838.7 25.3 %reduce-scatter.2.cloned.1.call-done = f32[96,2048]{1,0:T(8,128)} async-done(((f32[96,4096]{1,0:T(8,128)}), f32[96,2048]{1,0:T(8,128)}) %reduce-scatter.2.cloned.1.call-update) | async-done | bytes 786448 | tf_op jit(solution)/shard_map/reduce_scatter | solution.py:73
  864.0 0.0 copy-done.2
  864.0 1.9 select_bitcast_fusion
  (11 shorter events, 0.1 us)
Async XLA Ops:
  6.5 1.0 copy-start.4
  6.5 642.8 %all-gather.4.cloned.1.call-start = ((), (), s32[]{:S(2)}) async-start(), calls=%async_computation.3 | async-start | bytes 37748736 | tf_op jit(solution)/shard_map/all_gather | solution.py:20
  662.7 19.4 %copy-start.1 = (bf16[96,4096]{1,0:T(8,128)(2,1)}, bf16[96,4096]{1,0:T(8,128)(2,1)S(1)}, u32[]{:S(2)}) copy-start(bf16[96,4096]{1,0:T(8,128)(2,1)S(1)} %convolution_convert_fusion) | copy-start | bytes 2359300
  662.7 3.5 collective-permute-start
  669.6 5.1 copy-start.5
  669.6 5.2 copy-start.6
  669.6 143.9 %all-to-all-start = ((bf16[8,96,4096]{2,1,0:T(8,128)(2,1)}), bf16[8,96,4096]{2,1,0:T(8,128)(2,1)}, u32[]{:S(2)}, u32[]{:S(2)}) async-start(bf16[8,96,4096]{2,1,0:T(8,128)(2,1)} %stack.2), calls=%async_computation | async-start | bytes 12582912 | tf_op jit(solution)/shard_map/all_to_all | solution.py:47
  674.6 189.4 %reduce-scatter.2.cloned.1.call-start = ((), (), s32[]{:S(2)}) async-start(), calls=%async_computation.2 | async-start | bytes 2359296 | tf_op jit(solution)/shard_map/reduce_scatter | solution.py:73
  824.9 1.9 copy-start.3
  824.9 2.6 copy-start
  828.7 35.3 %copy-start.2 = (bf16[96,4096]{1,0:T(8,128)(2,1)S(1)}, bf16[96,4096]{1,0:T(8,128)(2,1)}, u32[]{:S(2)}) copy-start(bf16[96,4096]{1,0:T(8,128)(2,1)} %copy-done.1) | copy-start | bytes 2359300
Sparse Core Ops, SparseCore 0:
  8.9 640.3 all-gather.3
  838.9 25.0 reduce-scatter.1
